TPU v7x, 32 devices: a whole 2x2x4 slice. The times are simulated.
32 devices in a mesh: row: 16 (over z, y, core), col: 2 (over x).
Axes of the slice: x: 2, y: 2, z: 4, core: 2. Of those that a mesh axis runs over, the one named last changes fastest.
Arguments:
- layer_input: bfloat16 [16384, 1152], P(('row', 'col')), may hold values from -6 to 6
- attn_gain: bfloat16 [1152], replicated, may hold values from 0.099609375 to 1.8984375
- mlp_gain: bfloat16 [1152], replicated, may hold values from 0.099609375 to 1.8984375
- query_weight: bfloat16 [1152, 1152], P('row', 'col'), may hold values from -0.1875 to 0.1875
- key_weight: bfloat16 [1152, 384], P('row', 'col'), may hold values from -0.1875 to 0.1875
- value_weight: bfloat16 [1152, 384], P('row', 'col'), may hold values from -0.1875 to 0.1875
- out_weight: bfloat16 [1152, 1152], P('col', 'row'), may hold values from -4 to 4
- gate_weight: bfloat16 [1152, 3072], P('row', 'col'), may hold values from -0.1875 to 0.1875
- up_weight: bfloat16 [1152, 3072], P('row', 'col'), may hold values from -0.1875 to 0.1875
- down_weight: bfloat16 [3072, 1152], P('col', 'row'), may hold values from -0.109375 to 0.109375
- seq_ids: int32 [16384], P('row'), may hold values from 0 to 31, as said below
- block_ends: int32 [16384], P('row'), may hold values from 255 to 16383, as said below
- grad_output: bfloat16 [16384, 1152], P(('row', 'col')), may hold values from -6 to 6
Outputs:
- layer_output: bfloat16 [16384, 1152], P(('row', 'col'))
- grad_input: bfloat16 [16384, 1152], P(('row', 'col'))
- grad_attn_gain: float32 [1152], replicated
- grad_mlp_gain: float32 [1152], replicated
- grad_query: float32 [1152, 1152], P('row', 'col')
- grad_key: float32 [1152, 384], P('row', 'col')
- grad_value: float32 [1152, 384], P('row', 'col')
- grad_out_weight: float32 [1152, 1152], P('col', 'row')
- grad_gate: float32 [1152, 3072], P('row', 'col')
- grad_up: float32 [1152, 3072], P('row', 'col')
- grad_down: float32 [3072, 1152], P('col', 'row')
Inputs may be any that keep to these rules, and one draw needn't show every extreme that they name: `seq_ids`: ids never fall; span number s of the aligned spans of 1024 tokens holds exactly two sequences, with ids 2 * s and 2 * s + 1, each of 256 tokens or more. `block_ends`: values never fall; an attention block is a run of 1 to 256 tokens inside one sequence, and the first block of every sequence has exactly 256 tokens.
All inputs are finite; a program needn't handle non-finite values.
Results may differ from a plain program's by a relative error of at most 0.014.
The roundings to bfloat16 on the way count: a program that leaves them out, or rounds other values in their place, can miss the bound.
Values may be sent and summed in bfloat16 or wider, within the bound.
A program may use at most 192 MiB of HBM per device.

v0:
```python
import math
import jax
import jax.numpy as jnp
from jax import lax
from jax.sharding import PartitionSpec as P

QUERY_HEADS = 18
KEY_VALUE_HEADS = 6
HEAD_SIZE_DIM = 64
eps = 1e-05
rope_base = 10000.0
neg_fill = -1e30


def rotate_half(values, head_size):
    lane_index = jnp.arange(values.shape[-1], dtype=jnp.int32) % head_size
    forward_roll = jnp.roll(values, -(head_size // 2), axis=-1)
    backward_roll = jnp.roll(values, head_size // 2, axis=-1)
    return jnp.where(lane_index < head_size // 2, -forward_roll, backward_roll)


def rope_tables(position, table_width, head_size):
    lane_index = (jnp.arange(table_width, dtype=jnp.int32) % (head_size // 2)).astype(jnp.float32)
    frequency = jnp.exp(lane_index * (-2.0 * math.log(rope_base) / head_size))
    angles = position[:, None] * frequency[None, :]
    return (jnp.cos(angles), jnp.sin(angles))


def rotary(values, cosine, sine_part, head_size):
    return values * cosine + rotate_half(values, head_size) * sine_part


def rotary_back(upstream, cosine, sine_part, head_size):
    return upstream * cosine - rotate_half(upstream * sine_part, head_size)


def positions(seq_ids):
    token_index = jnp.arange(seq_ids.shape[0], dtype=jnp.int32)
    earlier = jnp.concatenate([seq_ids[:1] - 1, seq_ids[:-1]])
    seq_start = lax.cummax(jnp.where(seq_ids != earlier, token_index, 0), axis=0)
    return (token_index - seq_start).astype(jnp.float32)


def visible(query_seq, query_end, seq_ids, block_ends):
    return (query_seq[:, None] == seq_ids[None, :]) & (block_ends[None, :] <= query_end[:, None])


def to_rows(values):
    return lax.all_to_all(values, "col", split_axis=0, concat_axis=1, tiled=True)


def to_tokens(values):
    return lax.all_to_all(values, "col", split_axis=1, concat_axis=0, tiled=True)


def col_sums(values):
    return lax.psum_scatter(values, "col", scatter_dimension=0, tiled=True)


def widen(values):
    return lax.all_gather(values, "col", axis=0, tiled=True)


def shards(
    layer_input,
    attn_gain,
    mlp_gain,
    query_weight,
    key_weight,
    value_weight,
    out_weight,
    gate_weight,
    up_weight,
    down_weight,
    seq_ids,
    block_ends,
    grad_output,
):
    col_index = lax.axis_index("col")
    query_rows = layer_input.shape[0]
    block_rows = min(512, query_rows)
    block_count = query_rows // block_rows
    heads_per_group = QUERY_HEADS // KEY_VALUE_HEADS
    group_head_width = heads_per_group * HEAD_SIZE_DIM
    query_width = QUERY_HEADS * HEAD_SIZE_DIM
    score_scale = HEAD_SIZE_DIM ** (-0.5)
    attn_gain_float = attn_gain.astype(jnp.float32)
    mlp_gain_float = mlp_gain.astype(jnp.float32)
    full_input = lax.all_gather(layer_input, "col", axis=0, tiled=True)
    token_rows = full_input.shape[0]
    query_cols, key_cols, value_cols, out_rows, gate_cols, up_cols, down_rows = (
        lax.all_gather(query_weight, "row", axis=0, tiled=True),
        lax.all_gather(key_weight, "row", axis=0, tiled=True),
        lax.all_gather(value_weight, "row", axis=0, tiled=True),
        lax.all_gather(out_weight, "row", axis=1, tiled=True),
        lax.all_gather(gate_weight, "row", axis=0, tiled=True),
        lax.all_gather(up_weight, "row", axis=0, tiled=True),
        lax.all_gather(down_weight, "row", axis=1, tiled=True),
    )
    input_float = full_input.astype(jnp.float32)
    inv_all = lax.rsqrt(jnp.mean(input_float * input_float, axis=1, keepdims=True) + eps)
    attn_in = (input_float * inv_all * attn_gain_float).astype(jnp.bfloat16)
    query_unrotated = jnp.dot(attn_in, query_cols, preferred_element_type=jnp.float32).astype(
        jnp.bfloat16
    )
    key_raw = jnp.dot(attn_in, key_cols, preferred_element_type=jnp.float32).astype(jnp.bfloat16)
    value_projected = jnp.dot(attn_in, value_cols, preferred_element_type=jnp.float32).astype(
        jnp.bfloat16
    )
    query_all = to_rows(query_unrotated)
    key_all, value_all = (
        lax.all_gather(key_raw, "col", axis=1, tiled=True),
        lax.all_gather(value_projected, "col", axis=1, tiled=True),
    )
    position = positions(seq_ids)
    row_start = col_index * query_rows
    query_pos = lax.dynamic_slice_in_dim(position, row_start, query_rows)
    query_seq = lax.dynamic_slice_in_dim(seq_ids, row_start, query_rows)
    query_end = lax.dynamic_slice_in_dim(block_ends, row_start, query_rows)
    query_cos, query_sin = rope_tables(query_pos, query_width, HEAD_SIZE_DIM)
    key_cos, key_sin = rope_tables(position, key_all.shape[1], HEAD_SIZE_DIM)
    query_rotated = (
        rotary(query_all.astype(jnp.float32), query_cos, query_sin, HEAD_SIZE_DIM) * score_scale
    ).astype(jnp.bfloat16)
    key_rotated = rotary(key_all.astype(jnp.float32), key_cos, key_sin, HEAD_SIZE_DIM).astype(
        jnp.bfloat16
    )

    def block_inputs(block_index):
        first_row = block_index * block_rows
        allowed = visible(query_seq, query_end, seq_ids, block_ends)
        return (first_row, allowed)

    def group_scores(query_block, group_index, allowed):
        query_head_rows = lax.dynamic_slice_in_dim(
            query_block, group_index * group_head_width, group_head_width, 1
        ).reshape(block_rows, heads_per_group, HEAD_SIZE_DIM)
        key_group = lax.dynamic_slice_in_dim(
            key_rotated, group_index * HEAD_SIZE_DIM, HEAD_SIZE_DIM, 1
        )
        value_group = lax.dynamic_slice_in_dim(
            value_all, group_index * HEAD_SIZE_DIM, HEAD_SIZE_DIM, 1
        )
        scores = jnp.einsum(
            "qhd,kd->hqk", query_head_rows, key_group, preferred_element_type=jnp.float32
        )
        return (query_head_rows, key_group, value_group, jnp.where(allowed[None], scores, neg_fill))

    def attend_block(block_index):
        first_row, allowed = block_inputs(block_index)

        def attend_head_group(group_index):
            query_head_rows, key_group, value_group, scores = group_scores(
                query_rotated, group_index, allowed
            )
            row_top = jnp.max(scores, axis=2, keepdims=True)
            powers = jnp.exp(scores - row_top)
            exp_total = jnp.sum(powers, axis=2, keepdims=True)
            attn_probs = (powers / exp_total).astype(jnp.bfloat16)
            weighted_values = jnp.einsum(
                "hqk,kd->qhd", attn_probs, value_group, preferred_element_type=jnp.float32
            )
            return (
                weighted_values.reshape(block_rows, group_head_width),
                (row_top + jnp.log(exp_total))[:, :, 0],
            )

        weighted_value_rows, logsumexp_rows = lax.map(
            attend_head_group, jnp.arange(KEY_VALUE_HEADS, dtype=jnp.int32)
        )
        return (
            jnp.transpose(weighted_value_rows, (1, 0, 2)).reshape(block_rows, query_width),
            logsumexp_rows,
        )

    mixed_blocks, log_blocks = lax.map(attend_block, jnp.arange(block_count, dtype=jnp.int32))
    attn_rows = mixed_blocks.reshape(query_rows, query_width).astype(jnp.bfloat16)
    attn_tokens = to_tokens(attn_rows)
    attn_share = col_sums(jnp.dot(attn_tokens, out_rows, preferred_element_type=jnp.float32))
    residual = layer_input.astype(jnp.float32) + attn_share
    inv_two = lax.rsqrt(jnp.mean(residual * residual, axis=1, keepdims=True) + eps)
    normed_two = residual * inv_two
    mlp_in = widen((normed_two * mlp_gain_float).astype(jnp.bfloat16))
    gate_act = jnp.dot(mlp_in, gate_cols, preferred_element_type=jnp.float32)
    up_act = jnp.dot(mlp_in, up_cols, preferred_element_type=jnp.float32)
    hidden = (jax.nn.silu(gate_act) * up_act).astype(jnp.bfloat16)
    mlp_share = col_sums(jnp.dot(hidden, down_rows, preferred_element_type=jnp.float32))
    layer_output = (residual + mlp_share).astype(jnp.bfloat16)
    grad_float = grad_output.astype(jnp.float32)
    grad_full = widen(grad_output)
    grad_down = jnp.einsum("tf,td->fd", hidden, grad_full, preferred_element_type=jnp.float32)
    grad_hidden = jnp.einsum("td,fd->tf", grad_full, down_rows, preferred_element_type=jnp.float32)
    gate_sigmoid = jax.nn.sigmoid(gate_act)
    grad_gate_act = (
        grad_hidden * up_act * gate_sigmoid * (1.0 + gate_act * (1.0 - gate_sigmoid))
    ).astype(jnp.bfloat16)
    grad_up_act = (grad_hidden * gate_act * gate_sigmoid).astype(jnp.bfloat16)
    grad_gate = jnp.einsum("td,tf->df", mlp_in, grad_gate_act, preferred_element_type=jnp.float32)
    grad_up = jnp.einsum("td,tf->df", mlp_in, grad_up_act, preferred_element_type=jnp.float32)
    grad_mlp_share = col_sums(
        jnp.einsum("tf,df->td", grad_gate_act, gate_cols, preferred_element_type=jnp.float32)
        + jnp.einsum("tf,df->td", grad_up_act, up_cols, preferred_element_type=jnp.float32)
    )
    scaled_two = grad_mlp_share * mlp_gain_float
    inner_two = jnp.mean(scaled_two * normed_two, axis=1, keepdims=True)
    grad_residual = grad_float + inv_two * (scaled_two - normed_two * inner_two)
    grad_mlp_gain = jnp.sum(grad_mlp_share * normed_two, axis=0)
    grad_branch = grad_residual.astype(jnp.bfloat16)
    grad_attn_full = widen(grad_branch)
    grad_out_weight = jnp.einsum(
        "tq,td->qd", attn_tokens, grad_attn_full, preferred_element_type=jnp.float32
    )
    grad_mixture = to_rows(
        jnp.einsum(
            "td,qd->tq", grad_attn_full, out_rows, preferred_element_type=jnp.float32
        ).astype(jnp.bfloat16)
    )

    def back_block(carried_state, scan_items):
        block_index, block_log_total = scan_items
        first_row, allowed = block_inputs(block_index)

        def backward_head_group(inner_acc, group_items):
            group_index, log_group = group_items
            keys_acc, values_acc = inner_acc
            query_head_rows, key_group, value_group, scores = group_scores(
                query_rotated, group_index, allowed
            )
            attn_probs = jnp.exp(scores - log_group[:, :, None])
            grad_heads = lax.dynamic_slice_in_dim(
                grad_mixture, group_index * group_head_width, group_head_width, 1
            ).reshape(block_rows, heads_per_group, HEAD_SIZE_DIM)
            grad_probs = jnp.einsum(
                "qhd,kd->hqk", grad_heads, value_group, preferred_element_type=jnp.float32
            )
            value_piece = jnp.einsum(
                "hqk,qhd->kd",
                attn_probs.astype(jnp.bfloat16),
                grad_heads,
                preferred_element_type=jnp.float32,
            )
            inner_dot = jnp.sum(attn_probs * grad_probs, axis=2, keepdims=True)
            grad_scores = (attn_probs * (grad_probs - inner_dot)).astype(jnp.bfloat16)
            query_piece = jnp.einsum(
                "hqk,kd->qhd", grad_scores, key_group, preferred_element_type=jnp.float32
            ).reshape(block_rows, group_head_width)
            key_piece = jnp.einsum(
                "hqk,qhd->kd", grad_scores, query_head_rows, preferred_element_type=jnp.float32
            )
            column = group_index * HEAD_SIZE_DIM
            keys_acc = lax.dynamic_update_slice_in_dim(
                keys_acc,
                lax.dynamic_slice_in_dim(keys_acc, column, HEAD_SIZE_DIM, 1) + key_piece,
                column,
                1,
            )
            values_acc = lax.dynamic_update_slice_in_dim(
                values_acc,
                lax.dynamic_slice_in_dim(values_acc, column, HEAD_SIZE_DIM, 1) + value_piece,
                column,
                1,
            )
            return ((keys_acc, values_acc), query_piece)

        carried_state, query_pieces = lax.scan(
            backward_head_group,
            carried_state,
            (jnp.arange(KEY_VALUE_HEADS, dtype=jnp.int32), block_log_total),
        )
        return (
            carried_state,
            jnp.transpose(query_pieces, (1, 0, 2)).reshape(block_rows, query_width),
        )

    zeros_kv = jnp.zeros((token_rows, key_all.shape[1]), jnp.float32)
    (grad_keys, grad_values), query_blocks = lax.scan(
        back_block, (zeros_kv, zeros_kv), (jnp.arange(block_count, dtype=jnp.int32), log_blocks)
    )
    grad_query_rot = query_blocks.reshape(query_rows, query_width)
    grad_query_raw = to_tokens(
        rotary_back(grad_query_rot * score_scale, query_cos, query_sin, HEAD_SIZE_DIM).astype(
            jnp.bfloat16
        )
    )
    grad_key_part = rotary_back(grad_keys, key_cos, key_sin, HEAD_SIZE_DIM)
    grad_key_sum, grad_value_sum = (
        lax.psum_scatter(grad_key_part, "col", scatter_dimension=1, tiled=True),
        lax.psum_scatter(grad_values, "col", scatter_dimension=1, tiled=True),
    )
    grad_key_raw = grad_key_sum.astype(jnp.bfloat16)
    grad_value_raw = grad_value_sum.astype(jnp.bfloat16)
    grad_query = jnp.einsum(
        "td,tq->dq", attn_in, grad_query_raw, preferred_element_type=jnp.float32
    )
    grad_key = jnp.einsum("td,tq->dq", attn_in, grad_key_raw, preferred_element_type=jnp.float32)
    grad_value = jnp.einsum(
        "td,tq->dq", attn_in, grad_value_raw, preferred_element_type=jnp.float32
    )
    grad_attn_share = col_sums(
        jnp.einsum("tq,dq->td", grad_query_raw, query_cols, preferred_element_type=jnp.float32)
        + jnp.einsum("tq,dq->td", grad_key_raw, key_cols, preferred_element_type=jnp.float32)
        + jnp.einsum("tq,dq->td", grad_value_raw, value_cols, preferred_element_type=jnp.float32)
    )
    own_float = layer_input.astype(jnp.float32)
    inv_one = lax.rsqrt(jnp.mean(own_float * own_float, axis=1, keepdims=True) + eps)
    normed_one = own_float * inv_one
    scaled_one = grad_attn_share * attn_gain_float
    inner_one = jnp.mean(scaled_one * normed_one, axis=1, keepdims=True)
    grad_input = (grad_residual + inv_one * (scaled_one - normed_one * inner_one)).astype(
        jnp.bfloat16
    )
    grad_attn_gain = jnp.sum(grad_attn_share * normed_one, axis=0)
    weight_sums = (
        lax.psum_scatter(grad_query, "row", scatter_dimension=0, tiled=True),
        lax.psum_scatter(grad_key, "row", scatter_dimension=0, tiled=True),
        lax.psum_scatter(grad_value, "row", scatter_dimension=0, tiled=True),
        lax.psum_scatter(grad_out_weight, "row", scatter_dimension=1, tiled=True),
        lax.psum_scatter(grad_gate, "row", scatter_dimension=0, tiled=True),
        lax.psum_scatter(grad_up, "row", scatter_dimension=0, tiled=True),
        lax.psum_scatter(grad_down, "row", scatter_dimension=1, tiled=True),
    )
    gain_sums = lax.psum((grad_attn_gain, grad_mlp_gain), ("row", "col"))
    return (
        layer_output,
        grad_input,
        gain_sums[0],
        gain_sums[1],
        weight_sums[0],
        weight_sums[1],
        weight_sums[2],
        weight_sums[3],
        weight_sums[4],
        weight_sums[5],
        weight_sums[6],
    )


def solution(mesh):
    in_specs = (
        P(("row", "col"), None),
        P(),
        P(),
        P("row", "col"),
        P("row", "col"),
        P("row", "col"),
        P("col", "row"),
        P("row", "col"),
        P("row", "col"),
        P("col", "row"),
        P("row"),
        P("row"),
        P(("row", "col"), None),
    )
    out_specs = (
        P(("row", "col"), None),
        P(("row", "col"), None),
        P(),
        P(),
        P("row", "col"),
        P("row", "col"),
        P("row", "col"),
        P("col", "row"),
        P("row", "col"),
        P("row", "col"),
        P("col", "row"),
    )
    return jax.shard_map(shards, mesh=mesh, in_specs=in_specs, out_specs=out_specs, check_vma=False)
```

profile of v0, /device:TPU:0, one launch (start us, length us, event | category | flops | bytes accessed | tf_op | source)
XLA Modules:
  0.0 1523.2 jit_solution(14034235379282888117)
XLA Ops:
  14.5 24.8 %all_gather.42 = bf16[1152,192]{1,0:T(8,128)(2,1)S(1)} all-gather(bf16[72,192]{1,0:T(8,128)(2,1)S(1)} %copy-done.33), channel_id=1, replica_groups=mesh['row'=16,'col'=2] {'row'}, dimensions={0}, use_global_device_ids=true | all-gather | bytes 470016 | tf_op jit(solution)/shard_map/all_gather | solution.py:93
  39.4 19.0 %all_gather.40 = bf16[1152,192]{1,0:T(8,128)(2,1)S(1)} all-gather(bf16[72,192]{1,0:T(8,128)(2,1)S(1)} %copy-done.34), channel_id=1, replica_groups=mesh['row'=16,'col'=2] {'row'}, dimensions={0}, use_global_device_ids=true | all-gather | bytes 470016 | tf_op jit(solution)/shard_map/all_gather | solution.py:94
  126.8 62.2 %while.50 = (s32[]{:T(128)}, bf16[6,512,192]{1,2,0:T(8,128)(2,1)S(1)}, f32[6,3,512]{2,1,0:T(4,128)}, s32[6]{0:T(128)S(1)}, bf16[1024,384]{0,1:T(8,128)(2,1)}, /*...) while((s32[]{:T(128)}, ...), condition=%wide.region_6.7_spmd.clone.clone, body=%wide.region_3.6_spmd.clone.sunk.clone | while | flops 418380288 | bytes 22477056 | solution.py:168
  189.0 17.3 %all_to_all.64 = bf16[512,2,576]{0,2,1:T(8,128)(2,1)S(1)} all-to-all(bf16[512,2,576]{0,2,1:T(8,128)(2,1)S(1)} %bitcast.276), channel_id=1, replica_groups=mesh['row'=16,'col'=2] {'col'}, dimensions={1} | all-to-all | bytes 2359296 | tf_op jit(solution)/shard_map/all_to_all | solution.py:53
  214.1 56.8 %reduce-scatter.18.cloned.1.call-done = f32[512,1152]{1,0:T(8,128)} async-done(((f32[1024,1152]{1,0:T(8,128)}), f32[512,1152]{1,0:T(8,128)}) %reduce-scatter.18.cloned.1.call-update) | async-done | bytes 2359312 | tf_op jit(solution)/shard_map/reduce_scatter | solution.py:57
  277.9 42.6 %all-gather.20.cloned.1.call-done = bf16[1152,1536]{1,0:T(8,128)(2,1)} async-done(((bf16[72,1536]{1,0:T(8,128)(2,1)}), bf16[1152,1536]{1,0:T(8,128)(2,1)}) %all-gather.20.cloned.1.call-update) | async-done | bytes 3538960 | tf_op jit(solution)/shard_map/all_gather | solution.py:97
  320.5 37.1 %all-gather.16.cloned.1.call-done = bf16[1024,1152]{1,0:T(8,128)(2,1)} async-done(((bf16[512,1152]{1,0:T(8,128)(2,1)}), bf16[1024,1152]{1,0:T(8,128)(2,1)}) %all-gather.16.cloned.1.call-update) | async-done | bytes 2359312 | tf_op jit(solution)/shard_map/all_gather | solution.py:61
  367.3 40.2 %all-gather.18.cloned.1.call-done = bf16[1152,1536]{1,0:T(8,128)(2,1)} async-done(((bf16[72,1536]{1,0:T(8,128)(2,1)}), bf16[1152,1536]{1,0:T(8,128)(2,1)}) %all-gather.18.cloned.1.call-update) | async-done | bytes 3538960 | tf_op jit(solution)/shard_map/all_gather | solution.py:96
  417.1 27.0 %all-gather.24.cloned.1.call-done = bf16[1024,1152]{1,0:T(8,128)(2,1)} async-done(((bf16[512,1152]{1,0:T(8,128)(2,1)}), bf16[1024,1152]{1,0:T(8,128)(2,1)}) %all-gather.24.cloned.1.call-update) | async-done | bytes 2359312 | tf_op jit(solution)/shard_map/all_gather | solution.py:61
  444.1 49.8 %all-gather.22.cloned.1.call-done = bf16[1536,1152]{0,1:T(8,128)(2,1)} async-done(((bf16[1536,72]{0,1:T(8,128)(2,1)}), bf16[1536,1152]{0,1:T(8,128)(2,1)}) %all-gather.22.cloned.1.call-update) | async-done | bytes 3538960 | tf_op jit(solution)/shard_map/all_gather | solution.py:98
  516.8 59.1 %reduce-scatter.22.cloned.1.call-done = f32[512,1152]{1,0:T(8,128)} async-done(((f32[1024,1152]{1,0:T(8,128)}), f32[512,1152]{1,0:T(8,128)}) %reduce-scatter.22.cloned.1.call-update) | async-done | bytes 2359312 | tf_op jit(solution)/shard_map/reduce_scatter | solution.py:57
  581.8 36.2 %all-gather.26.cloned.1.call-done = bf16[1024,1152]{1,0:T(8,128)(2,1)} async-done(((bf16[512,1152]{1,0:T(8,128)(2,1)}), bf16[1024,1152]{1,0:T(8,128)(2,1)}) %all-gather.26.cloned.1.call-update) | async-done | bytes 2359312 | tf_op jit(solution)/shard_map/all_gather | solution.py:61
  627.7 15.1 all-to-all-done.2
  645.5 125.0 %while.51 = (s32[]{:T(128)}, f32[1024,384]{0,1:T(8,128)}, f32[1024,384]{0,1:T(8,128)}, f32[6,512,192]{1,2,0:T(8,128)}, s32[6]{0:T(128)S(1)}, /*index=5*/bf16[102...) while((s32[]{:T(128)}, f32[1024,384]{0,1:T(8,128)}, ...), condition=%wide.region_15.16_spmd.clone.clone, body=%wide.region_13.15_spmd.clone.sunk.clone | while | flops 1027209728 | bytes 55630144 | solution.py:265
  805.4 18.5 %all_to_all.65 = bf16[512,2,576]{0,2,1:T(8,128)(2,1)S(1)} all-to-all(bf16[512,2,576]{0,2,1:T(8,128)(2,1)S(1)} %subtract_convert_fusion), channel_id=1, replica_groups=mesh['row'=16,'col'=2] {'col'}, dimensions={1} | all-to-all | bytes 2359296 | tf_op jit(solution)/shard_map/all_to_all | solution.py:53
  909.8 40.1 %all-reduce.2 = (f32[1152]{0:T(1024)}, f32[1152]{0:T(1024)}) all-reduce(f32[1152]{0:T(1024)} %get-tuple-element.251, f32[1152]{0:T(1024)} %get-tuple-element.249), channel_id=1, replica_groups=mesh['row'=16,'col'=2] {'row','col'}, use_global_device_ids=true, to_apply=%region_21.22 | all-reduce | flops 2304 | bytes 18432 | tf_op jit(solution)/shard_map/psum | solution.py:322
  951.1 19.2 %reduce-scatter.20.cloned.1.call-done = f32[512,1152]{1,0:T(8,128)} async-done(((f32[1024,1152]{1,0:T(8,128)}), f32[512,1152]{1,0:T(8,128)}) %reduce-scatter.20.cloned.1.call-update) | async-done | bytes 2359312 | tf_op jit(solution)/shard_map/reduce_scatter | solution.py:57
  975.4 89.2 %reduce-scatter.38.cloned.1.call-done = f32[1536,72]{0,1:T(8,128)} async-done(((f32[1536,1152]{0,1:T(8,128)}), f32[1536,72]{0,1:T(8,128)}) %reduce-scatter.38.cloned.1.call-update) | async-done | bytes 442384 | tf_op jit(solution)/shard_map/reduce_scatter | solution.py:320
  1064.7 94.5 %reduce-scatter.36.cloned.1.call-done = f32[72,1536]{1,0:T(8,128)} async-done(((f32[1152,1536]{1,0:T(8,128)}), f32[72,1536]{1,0:T(8,128)}) %reduce-scatter.36.cloned.1.call-update) | async-done | bytes 442384 | tf_op jit(solution)/shard_map/reduce_scatter | solution.py:319
  1159.2 94.0 %reduce-scatter.34.cloned.1.call-done = f32[72,1536]{1,0:T(8,128)} async-done(((f32[1152,1536]{1,0:T(8,128)}), f32[72,1536]{1,0:T(8,128)}) %reduce-scatter.34.cloned.1.call-update) | async-done | bytes 442384 | tf_op jit(solution)/shard_map/reduce_scatter | solution.py:318
  1253.3 69.9 %reduce-scatter.42.cloned.1.call-done = f32[576,72]{0,1:T(8,128)} async-done(((f32[576,1152]{0,1:T(8,128)}), f32[576,72]{0,1:T(8,128)}) %reduce-scatter.42.cloned.1.call-update) | async-done | bytes 165904
  1323.1 61.6 %reduce-scatter.32.cloned.1.call-done = f32[72,192]{1,0:T(8,128)} async-done(((f32[1152,192]{1,0:T(8,128)}), f32[72,192]{1,0:T(8,128)}) %reduce-scatter.32.cloned.1.call-update) | async-done | bytes 55312 | tf_op jit(solution)/shard_map/reduce_scatter | solution.py:316
  1384.8 61.8 %reduce-scatter.30.cloned.1.call-done = f32[72,192]{1,0:T(8,128)} async-done(((f32[1152,192]{1,0:T(8,128)}), f32[72,192]{1,0:T(8,128)}) %reduce-scatter.30.cloned.1.call-update) | async-done | bytes 55312 | tf_op jit(solution)/shard_map/reduce_scatter | solution.py:315
  1446.6 69.3 %reduce-scatter.40.cloned.1.call-done = f32[72,576]{1,0:T(8,128)} async-done(((f32[1152,576]{1,0:T(8,128)}), f32[72,576]{1,0:T(8,128)}) %reduce-scatter.40.cloned.1.call-update) | async-done | bytes 165904
  (366 shorter events, 447.6 us)
Async XLA Ops:
  7.2 51.2 %all-gather.10.cloned.1.call-start = ((), (), s32[]{:S(2)}) async-start(), calls=%async_computation.17 | async-start | bytes 3538944 | tf_op jit(solution)/shard_map/all_gather | solution.py:89
  8.0 82.0 %all-gather.12.cloned.1.call-start = ((), (), s32[]{:S(2)}) async-start(), calls=%async_computation.18 | async-start | bytes 1566720 | tf_op jit(solution)/shard_map/all_gather | solution.py:92
  8.7 197.8 %all-gather.14.cloned.1.call-start = ((), (), s32[]{:S(2)}) async-start(), calls=%async_computation.19 | async-start | bytes 1566720 | tf_op jit(solution)/shard_map/all_gather | solution.py:95
  95.1 19.3 %all-to-all-start = ((bf16[2,512,576]{1,2,0:T(8,128)(2,1)}), bf16[2,512,576]{1,2,0:T(8,128)(2,1)S(1)}, u32[]{:S(2)}, u32[]{:S(2)}) async-start(bf16[2,512,576]{1,2,0:T(8,128)(2,1)} %bitcast.277), calls=%async_computation | async-start | bytes 2359296 | tf_op jit(solution)/shard_map/all_to_all | solution.py:49
  98.7 172.2 %reduce-scatter.18.cloned.1.call-start = ((), (), s32[]{:S(2)}) async-start(), calls=%async_computation.20 | async-start | bytes 7077888 | tf_op jit(solution)/shard_map/reduce_scatter | solution.py:57
  212.8 107.7 %all-gather.20.cloned.1.call-start = ((), (), s32[]{:S(2)}) async-start(), calls=%async_computation.23 | async-start | bytes 3760128 | tf_op jit(solution)/shard_map/all_gather | solution.py:97
  213.4 144.2 %all-gather.16.cloned.1.call-start = ((), (), s32[]{:S(2)}) async-start(), calls=%async_computation.21 | async-start | bytes 3538944 | tf_op jit(solution)/shard_map/all_gather | solution.py:61
  275.3 132.2 %all-gather.18.cloned.1.call-start = ((), (), s32[]{:S(2)}) async-start(), calls=%async_computation.22 | async-start | bytes 3760128 | tf_op jit(solution)/shard_map/all_gather | solution.py:96
  276.0 168.1 %all-gather.24.cloned.1.call-start = ((), (), s32[]{:S(2)}) async-start(), calls=%async_computation.26 | async-start | bytes 3538944 | tf_op jit(solution)/shard_map/all_gather | solution.py:61
  276.8 217.1 %all-gather.22.cloned.1.call-start = ((), (), s32[]{:S(2)}) async-start(), calls=%async_computation.24 | async-start | bytes 3760128 | tf_op jit(solution)/shard_map/all_gather | solution.py:98
  277.5 298.4 %reduce-scatter.22.cloned.1.call-start = ((), (), s32[]{:S(2)}) async-start(), calls=%async_computation.27 | async-start | bytes 7077888 | tf_op jit(solution)/shard_map/reduce_scatter | solution.py:57
  516.7 101.3 %all-gather.26.cloned.1.call-start = ((), (), s32[]{:S(2)}) async-start(), calls=%async_computation.28 | async-start | bytes 3538944 | tf_op jit(solution)/shard_map/all_gather | solution.py:61
  623.0 19.8 %all-to-all-start.2 = ((bf16[2,512,576]{1,2,0:T(8,128)(2,1)}), bf16[2,512,576]{1,2,0:T(8,128)(2,1)}, u32[]{:S(2)}, u32[]{:S(2)}) async-start(bf16[2,512,576]{1,2,0:T(8,128)(2,1)} %bitcast.162), calls=%async_computation.5 | async-start | bytes 2359296 | tf_op jit(solution)/shard_map/all_to_all | solution.py:49
  627.4 201.0 %reduce-scatter.24.cloned.1.call-start = ((), (), s32[]{:S(2)}) async-start(), calls=%async_computation.29 | async-start | bytes 2359296 | tf_op jit(solution)/shard_map/reduce_scatter | solution.py:287
  785.3 55.7 %reduce-scatter.26.cloned.1.call-start = ((), (), s32[]{:S(2)}) async-start(), calls=%async_computation.30 | async-start | bytes 2359296 | tf_op jit(solution)/shard_map/reduce_scatter | solution.py:288
  794.4 112.4 %reduce-scatter.28.cloned.1.call-start = ((), (), s32[]{:S(2)}) async-start(), calls=%async_computation.31 | async-start | bytes 7077888 | tf_op jit(solution)/shard_map/reduce_scatter | solution.py:57
  846.7 123.7 %reduce-scatter.20.cloned.1.call-start = ((), (), s32[]{:S(2)}) async-start(), calls=%async_computation.25 | async-start | bytes 7077888 | tf_op jit(solution)/shard_map/reduce_scatter | solution.py:57
  856.1 208.6 %reduce-scatter.38.cloned.1.call-start = ((), (), s32[]{:S(2)}) async-start(), calls=%async_computation.36 | async-start | bytes 7520256 | tf_op jit(solution)/shard_map/reduce_scatter | solution.py:320
  865.4 293.8 %reduce-scatter.36.cloned.1.call-start = ((), (), s32[]{:S(2)}) async-start(), calls=%async_computation.35 | async-start | bytes 7520256 | tf_op jit(solution)/shard_map/reduce_scatter | solution.py:319
  874.7 378.6 %reduce-scatter.34.cloned.1.call-start = ((), (), s32[]{:S(2)}) async-start(), calls=%async_computation.34 | async-start | bytes 7520256 | tf_op jit(solution)/shard_map/reduce_scatter | solution.py:318
  882.6 440.5 %reduce-scatter.42.cloned.1.call-start = ((), (), s32[]{:S(2)}) async-start(), calls=%async_computation.38 | async-start | bytes 3133440
  889.3 495.4 %reduce-scatter.32.cloned.1.call-start = ((), (), s32[]{:S(2)}) async-start(), calls=%async_computation.33 | async-start | bytes 1253376 | tf_op jit(solution)/shard_map/reduce_scatter | solution.py:316
  894.2 552.4 %reduce-scatter.30.cloned.1.call-start = ((), (), s32[]{:S(2)}) async-start(), calls=%async_computation.32 | async-start | bytes 1253376 | tf_op jit(solution)/shard_map/reduce_scatter | solution.py:315
  897.5 618.4 %reduce-scatter.40.cloned.1.call-start = ((), (), s32[]{:S(2)}) async-start(), calls=%async_computation.37 | async-start | bytes 3133440
  (59 other events, 1186.8 us)
Sparse Core Ops, SparseCore 0:
  9.6 38.7 all-gather.9
  50.6 39.3 all-gather.11
  92.1 38.1 all-gather.13
  212.9 57.8 reduce-scatter.17
  273.3 47.1 all-gather.19
  322.5 35.0 all-gather.15
  360.2 47.1 all-gather.17
  409.0 35.0 all-gather.23
  446.7 47.1 all-gather.21
  516.8 58.9 reduce-scatter.21
  582.0 36.0 all-gather.25
  785.4 26.4 reduce-scatter.23
  814.2 26.7 reduce-scatter.25
  846.8 59.9 reduce-scatter.27
  909.1 61.2 reduce-scatter.19
  974.8 89.8 reduce-scatter.37
  1069.6 89.5 reduce-scatter.35
  1163.7 89.5 reduce-scatter.33
  1258.3 64.8 reduce-scatter.41
  1327.6 57.0 reduce-scatter.31
  1389.4 57.1 reduce-scatter.29
  1451.6 64.2 reduce-scatter.39
where the time goes:
time: 1530 us; the launch traced here: 1520 us
  waiting for transfers between devices  949 us (62%)
  matrix products  228 us (15%)
  blocking collectives  143 us (9%)
  other arithmetic  115 us (8%)
  local copies, waits for them, and re-layouts  45.7 us (3%)
  loops' own time  16.1 us (1%)
  between operations  16.1 us (1%)
    unnamed x24, waiting for transfers between devices  144 us
    reduce_scatter x4, waiting for transfers between devices, col_sums(): return lax.psum_scatter(values, 'col', scatter_dimension=0, tiled=True)  139 us
    all_gather x3, waiting for transfers between devices, widen(): return lax.all_gather(values, 'col', axis=0, tiled=True)  100 us
    reduce_scatter x1, waiting for transfers between devices, shards(): lax.psum_scatter(grad_up, 'row', scatter_dimension=0, tiled=True)  94.5 us
    reduce_scatter x1, waiting for transfers between devices, shards(): lax.psum_scatter(grad_gate, 'row', scatter_dimension=0, tiled=True)  94 us
    reduce_scatter x1, waiting for transfers between devices, shards(): lax.psum_scatter(grad_down, 'row', scatter_dimension=1, tiled=True)  89.2 us
    reduce_scatter x1, waiting for transfers between devices, shards(): lax.psum_scatter(grad_key, 'row', scatter_dimension=0, tiled=True)  61.8 us
    reduce_scatter x1, waiting for transfers between devices, shards(): lax.psum_scatter(grad_value, 'row', scatter_dimension=0, tiled=True)  61.6 us
  transfers between devices with their start and end apart: 24, of which 21 were waited for; matrix products, arithmetic and copies ran while one was open for 13% of the time, Pallas kernels for 0%

commit v1 on v0

--- a/solution.py
+++ b/solution.py
@@ -319,7 +319,7 @@
         lax.psum_scatter(grad_up, "row", scatter_dimension=0, tiled=True),
         lax.psum_scatter(grad_down, "row", scatter_dimension=1, tiled=True),
     )
-    gain_sums = lax.psum((grad_attn_gain, grad_mlp_gain), ("row", "col"))
+    gain_sums = lax.psum(lax.psum((grad_attn_gain, grad_mlp_gain), "col"), "row")
     return (
         layer_output,
         grad_input,

time: 1530 us -> 1530 us (level)
  waiting for transfers between devices: 949 us -> 920 us
  blocking collectives: 143 us -> 171 us
    psum x1 -> x2, blocking collectives: 40.1 us -> 67.7 us  [the longest x1 59.5 us: shards(): lax.psum(lax.psum((grad_attn_gain, grad_mlp_gain), 'col'), 'row')]
    reduce_scatter x4, waiting for transfers between devices: 139 us -> 120 us  [col_sums(): return lax.psum_scatter(values, 'col', scatter_dimension=0, tiled=True)]
  transfers between devices with their start and end apart: 24 -> 24, of which waited for: 21 -> 20; matrix products, arithmetic and copies ran while one was open for 13% -> 13% of each run, Pallas kernels for 0% -> 0%
where the time goes in v1:
time: 1530 us; the launch traced here: 1520 us
  waiting for transfers between devices  920 us (60%)
  matrix products  227 us (15%)
  blocking collectives  171 us (11%)
  other arithmetic  116 us (8%)
  local copies, waits for them, and re-layouts  45.6 us (3%)
  loops' own time  16.1 us (1%)
  between operations  16.1 us (1%)
    unnamed x24, waiting for transfers between devices  144 us
    reduce_scatter x4, waiting for transfers between devices, col_sums(): return lax.psum_scatter(values, 'col', scatter_dimension=0, tiled=True)  120 us
    all_gather x3, waiting for transfers between devices, widen(): return lax.all_gather(values, 'col', axis=0, tiled=True)  100 us
    reduce_scatter x1, waiting for transfers between devices, shards(): lax.psum_scatter(grad_up, 'row', scatter_dimension=0, tiled=True)  94.6 us
    reduce_scatter x1, waiting for transfers between devices, shards(): lax.psum_scatter(grad_gate, 'row', scatter_dimension=0, tiled=True)  94 us
    reduce_scatter x1, waiting for transfers between devices, shards(): lax.psum_scatter(grad_down, 'row', scatter_dimension=1, tiled=True)  79.3 us
    reduce_scatter x1, waiting for transfers between devices, shards(): lax.psum_scatter(grad_key, 'row', scatter_dimension=0, tiled=True)  61.7 us
    reduce_scatter x1, waiting for transfers between devices, shards(): lax.psum_scatter(grad_value, 'row', scatter_dimension=0, tiled=True)  61.6 us
  transfers between devices with their start and end apart: 24, of which 20 were waited for; matrix products, arithmetic and copies ran while one was open for 13% of the time, Pallas kernels for 0%

profile of v1, /device:TPU:0, one launch (start us, length us, event | category | flops | bytes accessed | tf_op | source)
XLA Modules:
  0.0 1521.9 jit_solution(14098197420800026804)
XLA Ops:
  14.5 24.8 %all_gather.42 = bf16[1152,192]{1,0:T(8,128)(2,1)S(1)} all-gather(bf16[72,192]{1,0:T(8,128)(2,1)S(1)} %copy-done.33), channel_id=1, replica_groups=mesh['row'=16,'col'=2] {'row'}, dimensions={0}, use_global_device_ids=true | all-gather | bytes 470016 | tf_op jit(solution)/shard_map/all_gather | solution.py:93
  39.4 19.0 %all_gather.40 = bf16[1152,192]{1,0:T(8,128)(2,1)S(1)} all-gather(bf16[72,192]{1,0:T(8,128)(2,1)S(1)} %copy-done.34), channel_id=1, replica_groups=mesh['row'=16,'col'=2] {'row'}, dimensions={0}, use_global_device_ids=true | all-gather | bytes 470016 | tf_op jit(solution)/shard_map/all_gather | solution.py:94
  126.8 62.2 %while.50 = (s32[]{:T(128)}, bf16[6,512,192]{1,2,0:T(8,128)(2,1)S(1)}, f32[6,3,512]{2,1,0:T(4,128)}, s32[6]{0:T(128)S(1)}, bf16[1024,384]{0,1:T(8,128)(2,1)}, /*...) while((s32[]{:T(128)}, ...), condition=%wide.region_6.7_spmd.clone.clone, body=%wide.region_3.6_spmd.clone.sunk.clone | while | flops 418380288 | bytes 22477056 | solution.py:168
  189.0 17.3 %all_to_all.64 = bf16[512,2,576]{0,2,1:T(8,128)(2,1)S(1)} all-to-all(bf16[512,2,576]{0,2,1:T(8,128)(2,1)S(1)} %bitcast.276), channel_id=1, replica_groups=mesh['row'=16,'col'=2] {'col'}, dimensions={1} | all-to-all | bytes 2359296 | tf_op jit(solution)/shard_map/all_to_all | solution.py:53
  214.1 56.8 %reduce-scatter.18.cloned.1.call-done = f32[512,1152]{1,0:T(8,128)} async-done(((f32[1024,1152]{1,0:T(8,128)}), f32[512,1152]{1,0:T(8,128)}) %reduce-scatter.18.cloned.1.call-update) | async-done | bytes 2359312 | tf_op jit(solution)/shard_map/reduce_scatter | solution.py:57
  277.9 42.6 %all-gather.20.cloned.1.call-done = bf16[1152,1536]{1,0:T(8,128)(2,1)} async-done(((bf16[72,1536]{1,0:T(8,128)(2,1)}), bf16[1152,1536]{1,0:T(8,128)(2,1)}) %all-gather.20.cloned.1.call-update) | async-done | bytes 3538960 | tf_op jit(solution)/shard_map/all_gather | solution.py:97
  320.5 37.1 %all-gather.16.cloned.1.call-done = bf16[1024,1152]{1,0:T(8,128)(2,1)} async-done(((bf16[512,1152]{1,0:T(8,128)(2,1)}), bf16[1024,1152]{1,0:T(8,128)(2,1)}) %all-gather.16.cloned.1.call-update) | async-done | bytes 2359312 | tf_op jit(solution)/shard_map/all_gather | solution.py:61
  367.2 40.2 %all-gather.18.cloned.1.call-done = bf16[1152,1536]{1,0:T(8,128)(2,1)} async-done(((bf16[72,1536]{1,0:T(8,128)(2,1)}), bf16[1152,1536]{1,0:T(8,128)(2,1)}) %all-gather.18.cloned.1.call-update) | async-done | bytes 3538960 | tf_op jit(solution)/shard_map/all_gather | solution.py:96
  417.1 27.0 %all-gather.24.cloned.1.call-done = bf16[1024,1152]{1,0:T(8,128)(2,1)} async-done(((bf16[512,1152]{1,0:T(8,128)(2,1)}), bf16[1024,1152]{1,0:T(8,128)(2,1)}) %all-gather.24.cloned.1.call-update) | async-done | bytes 2359312 | tf_op jit(solution)/shard_map/all_gather | solution.py:61
  444.1 49.8 %all-gather.22.cloned.1.call-done = bf16[1536,1152]{0,1:T(8,128)(2,1)} async-done(((bf16[1536,72]{0,1:T(8,128)(2,1)}), bf16[1536,1152]{0,1:T(8,128)(2,1)}) %all-gather.22.cloned.1.call-update) | async-done | bytes 3538960 | tf_op jit(solution)/shard_map/all_gather | solution.py:98
  493.9 12.4 multiply_convert_fusion
  516.7 59.1 %reduce-scatter.22.cloned.1.call-done = f32[512,1152]{1,0:T(8,128)} async-done(((f32[1024,1152]{1,0:T(8,128)}), f32[512,1152]{1,0:T(8,128)}) %reduce-scatter.22.cloned.1.call-update) | async-done | bytes 2359312 | tf_op jit(solution)/shard_map/reduce_scatter | solution.py:57
  581.6 36.3 %all-gather.26.cloned.1.call-done = bf16[1024,1152]{1,0:T(8,128)(2,1)} async-done(((bf16[512,1152]{1,0:T(8,128)(2,1)}), bf16[1024,1152]{1,0:T(8,128)(2,1)}) %all-gather.26.cloned.1.call-update) | async-done | bytes 2359312 | tf_op jit(solution)/shard_map/all_gather | solution.py:61
  627.5 15.1 all-to-all-done.2
  645.3 125.1 %while.51 = (s32[]{:T(128)}, f32[1024,384]{0,1:T(8,128)}, f32[1024,384]{0,1:T(8,128)}, f32[6,512,192]{1,2,0:T(8,128)}, s32[6]{0:T(128)S(1)}, /*index=5*/bf16[102...) while((s32[]{:T(128)}, f32[1024,384]{0,1:T(8,128)}, ...), condition=%wide.region_15.16_spmd.clone.clone, body=%wide.region_13.15_spmd.clone.sunk.clone | while | flops 1027209728 | bytes 55630144 | solution.py:265
  805.2 18.5 %all_to_all.65 = bf16[512,2,576]{0,2,1:T(8,128)(2,1)S(1)} all-to-all(bf16[512,2,576]{0,2,1:T(8,128)(2,1)S(1)} %subtract_convert_fusion), channel_id=1, replica_groups=mesh['row'=16,'col'=2] {'col'}, dimensions={1} | all-to-all | bytes 2359296 | tf_op jit(solution)/shard_map/all_to_all | solution.py:53
  917.8 59.5 %all-reduce.2 = (f32[1152]{0:T(1024)}, f32[1152]{0:T(1024)}) all-reduce(f32[1152]{0:T(1024)} %get-tuple-element.305, f32[1152]{0:T(1024)} %get-tuple-element.306), channel_id=1, replica_groups=mesh['row'=16,'col'=2] {'row'}, use_global_device_ids=true, to_apply=%region_22.23 | all-reduce | flops 2304 | bytes 18432 | tf_op jit(solution)/shard_map/psum | solution.py:322
  984.2 79.3 %reduce-scatter.38.cloned.1.call-done = f32[1536,72]{0,1:T(8,128)} async-done(((f32[1536,1152]{0,1:T(8,128)}), f32[1536,72]{0,1:T(8,128)}) %reduce-scatter.38.cloned.1.call-update) | async-done | bytes 442384 | tf_op jit(solution)/shard_map/reduce_scatter | solution.py:320
  1063.5 94.6 %reduce-scatter.36.cloned.1.call-done = f32[72,1536]{1,0:T(8,128)} async-done(((f32[1152,1536]{1,0:T(8,128)}), f32[72,1536]{1,0:T(8,128)}) %reduce-scatter.36.cloned.1.call-update) | async-done | bytes 442384 | tf_op jit(solution)/shard_map/reduce_scatter | solution.py:319
  1158.1 94.0 %reduce-scatter.34.cloned.1.call-done = f32[72,1536]{1,0:T(8,128)} async-done(((f32[1152,1536]{1,0:T(8,128)}), f32[72,1536]{1,0:T(8,128)}) %reduce-scatter.34.cloned.1.call-update) | async-done | bytes 442384 | tf_op jit(solution)/shard_map/reduce_scatter | solution.py:318
  1252.1 69.8 %reduce-scatter.42.cloned.1.call-done = f32[576,72]{0,1:T(8,128)} async-done(((f32[576,1152]{0,1:T(8,128)}), f32[576,72]{0,1:T(8,128)}) %reduce-scatter.42.cloned.1.call-update) | async-done | bytes 165904
  1321.9 61.6 %reduce-scatter.32.cloned.1.call-done = f32[72,192]{1,0:T(8,128)} async-done(((f32[1152,192]{1,0:T(8,128)}), f32[72,192]{1,0:T(8,128)}) %reduce-scatter.32.cloned.1.call-update) | async-done | bytes 55312 | tf_op jit(solution)/shard_map/reduce_scatter | solution.py:316
  1383.6 61.7 %reduce-scatter.30.cloned.1.call-done = f32[72,192]{1,0:T(8,128)} async-done(((f32[1152,192]{1,0:T(8,128)}), f32[72,192]{1,0:T(8,128)}) %reduce-scatter.30.cloned.1.call-update) | async-done | bytes 55312 | tf_op jit(solution)/shard_map/reduce_scatter | solution.py:315
  1445.3 69.3 %reduce-scatter.40.cloned.1.call-done = f32[72,576]{1,0:T(8,128)} async-done(((f32[1152,576]{1,0:T(8,128)}), f32[72,576]{1,0:T(8,128)}) %reduce-scatter.40.cloned.1.call-update) | async-done | bytes 165904
  (367 shorter events, 443.7 us)
Async XLA Ops:
  7.2 51.2 %all-gather.10.cloned.1.call-start = ((), (), s32[]{:S(2)}) async-start(), calls=%async_computation.17 | async-start | bytes 3538944 | tf_op jit(solution)/shard_map/all_gather | solution.py:89
  8.0 82.0 %all-gather.12.cloned.1.call-start = ((), (), s32[]{:S(2)}) async-start(), calls=%async_computation.18 | async-start | bytes 1566720 | tf_op jit(solution)/shard_map/all_gather | solution.py:92
  8.7 197.8 %all-gather.14.cloned.1.call-start = ((), (), s32[]{:S(2)}) async-start(), calls=%async_computation.19 | async-start | bytes 1566720 | tf_op jit(solution)/shard_map/all_gather | solution.py:95
  95.1 19.3 %all-to-all-start = ((bf16[2,512,576]{1,2,0:T(8,128)(2,1)}), bf16[2,512,576]{1,2,0:T(8,128)(2,1)S(1)}, u32[]{:S(2)}, u32[]{:S(2)}) async-start(bf16[2,512,576]{1,2,0:T(8,128)(2,1)} %bitcast.277), calls=%async_computation | async-start | bytes 2359296 | tf_op jit(solution)/shard_map/all_to_all | solution.py:49
  98.7 172.2 %reduce-scatter.18.cloned.1.call-start = ((), (), s32[]{:S(2)}) async-start(), calls=%async_computation.20 | async-start | bytes 7077888 | tf_op jit(solution)/shard_map/reduce_scatter | solution.py:57
  212.8 107.7 %all-gather.20.cloned.1.call-start = ((), (), s32[]{:S(2)}) async-start(), calls=%async_computation.23 | async-start | bytes 3760128 | tf_op jit(solution)/shard_map/all_gather | solution.py:97
  213.4 144.2 %all-gather.16.cloned.1.call-start = ((), (), s32[]{:S(2)}) async-start(), calls=%async_computation.21 | async-start | bytes 3538944 | tf_op jit(solution)/shard_map/all_gather | solution.py:61
  275.2 132.2 %all-gather.18.cloned.1.call-start = ((), (), s32[]{:S(2)}) async-start(), calls=%async_computation.22 | async-start | bytes 3760128 | tf_op jit(solution)/shard_map/all_gather | solution.py:96
  276.0 168.1 %all-gather.24.cloned.1.call-start = ((), (), s32[]{:S(2)}) async-start(), calls=%async_computation.26 | async-start | bytes 3538944 | tf_op jit(solution)/shard_map/all_gather | solution.py:61
  276.7 217.1 %all-gather.22.cloned.1.call-start = ((), (), s32[]{:S(2)}) async-start(), calls=%async_computation.24 | async-start | bytes 3760128 | tf_op jit(solution)/shard_map/all_gather | solution.py:98
  277.5 298.2 %reduce-scatter.22.cloned.1.call-start = ((), (), s32[]{:S(2)}) async-start(), calls=%async_computation.27 | async-start | bytes 7077888 | tf_op jit(solution)/shard_map/reduce_scatter | solution.py:57
  516.6 101.3 %all-gather.26.cloned.1.call-start = ((), (), s32[]{:S(2)}) async-start(), calls=%async_computation.28 | async-start | bytes 3538944 | tf_op jit(solution)/shard_map/all_gather | solution.py:61
  622.8 19.8 %all-to-all-start.2 = ((bf16[2,512,576]{1,2,0:T(8,128)(2,1)}), bf16[2,512,576]{1,2,0:T(8,128)(2,1)}, u32[]{:S(2)}, u32[]{:S(2)}) async-start(bf16[2,512,576]{1,2,0:T(8,128)(2,1)} %bitcast.162), calls=%async_computation.5 | async-start | bytes 2359296 | tf_op jit(solution)/shard_map/all_to_all | solution.py:49
  627.2 201.0 %reduce-scatter.24.cloned.1.call-start = ((), (), s32[]{:S(2)}) async-start(), calls=%async_computation.29 | async-start | bytes 2359296 | tf_op jit(solution)/shard_map/reduce_scatter | solution.py:287
  785.1 55.7 %reduce-scatter.26.cloned.1.call-start = ((), (), s32[]{:S(2)}) async-start(), calls=%async_computation.30 | async-start | bytes 2359296 | tf_op jit(solution)/shard_map/reduce_scatter | solution.py:288
  794.2 112.4 %reduce-scatter.28.cloned.1.call-start = ((), (), s32[]{:S(2)}) async-start(), calls=%async_computation.31 | async-start | bytes 7077888 | tf_op jit(solution)/shard_map/reduce_scatter | solution.py:57
  846.4 132.1 %reduce-scatter.20.cloned.1.call-start = ((), (), s32[]{:S(2)}) async-start(), calls=%async_computation.25 | async-start | bytes 7077888 | tf_op jit(solution)/shard_map/reduce_scatter | solution.py:57
  855.9 207.6 %reduce-scatter.38.cloned.1.call-start = ((), (), s32[]{:S(2)}) async-start(), calls=%async_computation.36 | async-start | bytes 7520256 | tf_op jit(solution)/shard_map/reduce_scatter | solution.py:320
  865.2 292.8 %reduce-scatter.36.cloned.1.call-start = ((), (), s32[]{:S(2)}) async-start(), calls=%async_computation.35 | async-start | bytes 7520256 | tf_op jit(solution)/shard_map/reduce_scatter | solution.py:319
  874.5 377.6 %reduce-scatter.34.cloned.1.call-start = ((), (), s32[]{:S(2)}) async-start(), calls=%async_computation.34 | async-start | bytes 7520256 | tf_op jit(solution)/shard_map/reduce_scatter | solution.py:318
  882.4 439.5 %reduce-scatter.42.cloned.1.call-start = ((), (), s32[]{:S(2)}) async-start(), calls=%async_computation.38 | async-start | bytes 3133440
  889.1 494.5 %reduce-scatter.32.cloned.1.call-start = ((), (), s32[]{:S(2)}) async-start(), calls=%async_computation.33 | async-start | bytes 1253376 | tf_op jit(solution)/shard_map/reduce_scatter | solution.py:316
  894.0 551.4 %reduce-scatter.30.cloned.1.call-start = ((), (), s32[]{:S(2)}) async-start(), calls=%async_computation.32 | async-start | bytes 1253376 | tf_op jit(solution)/shard_map/reduce_scatter | solution.py:315
  897.3 617.3 %reduce-scatter.40.cloned.1.call-start = ((), (), s32[]{:S(2)}) async-start(), calls=%async_computation.37 | async-start | bytes 3133440
  (59 other events, 1203.3 us)
Sparse Core Ops, SparseCore 0:
  9.6 38.7 all-gather.9
  50.6 39.3 all-gather.11
  92.1 38.1 all-gather.13
  212.9 57.8 reduce-scatter.17
  273.3 47.1 all-gather.19
  322.5 35.0 all-gather.15
  360.2 47.1 all-gather.17
  409.0 35.0 all-gather.23
  446.7 47.1 all-gather.21
  516.7 58.9 reduce-scatter.21
  581.7 36.0 all-gather.25
  785.2 26.4 reduce-scatter.23
  814.0 26.7 reduce-scatter.25
  846.6 59.9 reduce-scatter.27
  908.9 60.0 reduce-scatter.19
  973.4 90.0 reduce-scatter.37
  1068.5 89.5 reduce-scatter.35
  1162.5 89.5 reduce-scatter.33
  1257.1 64.7 reduce-scatter.41
  1326.4 57.1 reduce-scatter.31
  1388.2 57.0 reduce-scatter.29
  1450.3 64.2 reduce-scatter.39
